TPU v7x, 256 devices: a whole 4x4x8 slice. The times are simulated.
256 devices in a mesh: sp: 8 (over z), dp: 32 (over x, y, core).
Axes of the slice: x: 4, y: 4, z: 8, core: 2. Of those that a mesh axis runs over, the one named last changes fastest.
Arguments:
- hidden_states: bfloat16 [32, 2048, 8192], P('dp', 'sp'), may hold values from -6 to 6
- queries: bfloat16 [32, 2048, 4096], P('dp', 'sp'), may hold values from -360 to 360
- norm_gain: bfloat16 [8192], replicated, may hold values from 0.5 to 1.5
- key_value_matrix: bfloat16 [8192, 1024], P('dp'), may hold values from -0.0625 to 0.0625
- trace_offsets: int32 [32, 9], P('dp'), may hold values from 0 to 2048, as said below
- token_order: int32 [32, 2048], P('dp'), may hold values from 0 to 2047, each once within a row
Outputs:
- attended: bfloat16 [32, 2048, 4096], P('dp', 'sp')
Inputs may be any that keep to these rules, and one draw needn't show every extreme that they name: Each row rises strictly from 0 to 2048; trace t of pack p holds the positions from trace_offsets[p, t] to trace_offsets[p, t + 1] - 1. `token_order`: each row is a permutation of the 2048 positions of its pack.
All inputs are finite; a program needn't handle non-finite values.
Results may differ from a plain program's by a relative error of at most 0.0034.
The roundings to bfloat16 on the way count: a program that leaves them out, or rounds other values in their place, can miss the bound.
Values may be sent and summed in bfloat16 or wider, within the bound.
No kernel may reach another device: no remote copies, remote signals or barrier semaphores. Data moves between devices by JAX's collectives and lax.ppermute only.
A program may use at most 128 MiB of HBM per device.

v0:
```python
import math
import jax
import jax.numpy as jnp
from jax import lax
from jax.sharding import PartitionSpec as P

QUERY_HEADS = 32
KEY_VALUE_HEADS = 4
HEAD_SIZE = 128
EPSILON = 1e-05
ROPE_BASE = 500000.0


def locate(positions, starts):
    inside = starts[None, :] <= positions[:, None]
    trace_ids = jnp.sum(inside.astype(jnp.int32), axis=1) - 1
    begin = jnp.max(jnp.where(inside, starts[None, :], 0), axis=1)
    return (trace_ids, positions - begin)


def rotate(vectors, within):
    half = vectors.shape[-1] // 2
    index = jnp.arange(half, dtype=jnp.float32)
    freqs = jnp.exp(index * (-2.0 * math.log(ROPE_BASE) / vectors.shape[-1]))
    angles = within.astype(jnp.float32)[:, None] * freqs[None, :]
    cosine = jnp.cos(angles)[:, None, :]
    sine = jnp.sin(angles)[:, None, :]
    first = vectors[..., :half]
    second = vectors[..., half:]
    return jnp.concatenate(
        [first * cosine - second * sine, second * cosine + first * sine], axis=-1
    )


def normalize(rows, gain):
    value_rows = rows.astype(jnp.float32)
    scale = lax.rsqrt(jnp.mean(value_rows * value_rows, axis=-1, keepdims=True) + EPSILON)
    return (value_rows * scale * gain.astype(jnp.float32)).astype(jnp.bfloat16)


def on_device(hidden_states, queries, norm_gain, key_value_matrix, trace_offsets, token_order):
    sequence_parallel_count = lax.axis_size("sp")
    my_index = lax.axis_index("sp")
    resident_rows = hidden_states.shape[1]
    all_rows = resident_rows * sequence_parallel_count
    normed = normalize(hidden_states[0], norm_gain)
    projected_rows = jnp.dot(
        normed,
        lax.all_gather(key_value_matrix, "dp", axis=0, tiled=True),
        preferred_element_type=jnp.float32,
    )
    starts = trace_offsets[0]
    positions = token_order[0]
    trace_ids, within = locate(positions, starts)
    own_within = lax.dynamic_slice_in_dim(within, my_index * resident_rows, resident_rows, 0)
    head_slices = rotate(
        queries[0].astype(jnp.float32).reshape(resident_rows, QUERY_HEADS, HEAD_SIZE), own_within
    ).astype(jnp.bfloat16)
    key_value_pairs = projected_rows.reshape(resident_rows, KEY_VALUE_HEADS, 2, HEAD_SIZE)
    key_rows = rotate(key_value_pairs[:, :, 0], own_within).astype(jnp.bfloat16)
    value_rows = key_value_pairs[:, :, 1].astype(jnp.bfloat16)
    query_groups = max(KEY_VALUE_HEADS, sequence_parallel_count)
    stacked_rows = jnp.repeat(
        jnp.stack((key_rows, value_rows), axis=2), query_groups // KEY_VALUE_HEADS, axis=1
    ).reshape(resident_rows, query_groups * 2 * HEAD_SIZE)
    moved_queries, moved_pairs = (
        lax.all_to_all(
            head_slices.reshape(resident_rows, QUERY_HEADS * HEAD_SIZE),
            "sp",
            split_axis=1,
            concat_axis=0,
            tiled=True,
        ),
        lax.all_to_all(stacked_rows, "sp", split_axis=1, concat_axis=0, tiled=True),
    )
    local_groups = query_groups // sequence_parallel_count
    local_heads = QUERY_HEADS // sequence_parallel_count
    per_group = local_heads // local_groups
    moved_queries = moved_queries.reshape(all_rows, local_groups, per_group, HEAD_SIZE)
    moved_pairs = moved_pairs.reshape(all_rows, local_groups, 2, HEAD_SIZE)
    keys_all = moved_pairs[:, :, 0]
    values_all = moved_pairs[:, :, 1]
    width = min(512, all_rows)

    def block(block_index):
        first_row = block_index * width
        query_block = lax.dynamic_slice_in_dim(moved_queries, first_row, width, 0)
        block_ids = lax.dynamic_slice_in_dim(trace_ids, first_row, width, 0)
        block_positions = lax.dynamic_slice_in_dim(positions, first_row, width, 0)
        scores = jnp.einsum(
            "bgpd,kgd->gpbk", query_block, keys_all, preferred_element_type=jnp.float32
        ) / math.sqrt(HEAD_SIZE)
        mask = (block_ids[:, None] == trace_ids[None, :]) & (
            positions[None, :] <= block_positions[:, None]
        )
        scores = jnp.where(mask, scores, -1e30)
        peak = jnp.max(scores, axis=-1, keepdims=True)
        expo = jnp.where(mask, jnp.exp(scores - peak), 0.0)
        totals = jnp.sum(expo, axis=-1)
        weights = expo.astype(jnp.bfloat16)
        mixed = jnp.einsum(
            "gpbk,kgd->bgpd", weights, values_all, preferred_element_type=jnp.float32
        )
        result = mixed / jnp.transpose(totals, (2, 0, 1))[..., None]
        return result.astype(jnp.bfloat16).reshape(width, local_heads * HEAD_SIZE)

    attended = lax.map(block, jnp.arange(all_rows // width, dtype=jnp.int32)).reshape(
        all_rows, local_heads * HEAD_SIZE
    )
    returned = lax.all_to_all(attended, "sp", split_axis=0, concat_axis=1, tiled=True)
    return returned[None]


def solution(mesh):
    return jax.shard_map(
        on_device,
        mesh=mesh,
        in_specs=(
            P("dp", "sp", None),
            P("dp", "sp", None),
            P(),
            P("dp", None),
            P("dp", None),
            P("dp", None),
        ),
        out_specs=P("dp", "sp", None),
        check_vma=False,
    )
```

profile of v0, /device:TPU:1, one launch (start us, length us, event | category | flops | bytes accessed | tf_op | source)
XLA Modules:
  0.0 302.1 jit_solution(7556706558653838073)
XLA Ops:
  7.3 4.3 %copy.44 = f32[1,256,4096]{1,2,0:T(8,128)} copy(bf16[1,256,4096]{2,1,0:T(8,128)(2,1)} %param.9) | data formatting | bytes 6291456 | tf_op jit(solution)/shard_map/convert_element_type | solution.py:57
  16.6 9.0 %all-to-all-start = ((bf16[256,8,512]{0,2,1:T(8,128)(2,1)}), bf16[256,8,512]{0,2,1:T(8,128)(2,1)S(1)}, u32[]{:S(2)}, u32[]{:S(2)}) async-start(bf16[256,8,512]{0,2,1:T(8,128)(2,1)} %bitcast.126), calls=%async_computation | async-start | bytes 4194304 | tf_op jit(solution)/shard_map/all_to_all | solution.py:67
  25.6 3.4 %fusion.21 = f32[256]{0:T(256)S(1)} fusion(bf16[1,256,8192]{2,1,0:T(8,128)(2,1)} %param.8), kind=kLoop, calls=%fused_computation.23 | loop fusion | flops 6291200 | bytes 4195328 | tf_op jit(solution)/shard_map/reduce_sum | solution.py:37
  29.0 62.8 %all-gather.2.cloned.1.call-done = bf16[8192,1024]{1,0:T(8,128)(2,1)} async-done(((bf16[256,1024]{1,0:T(8,128)(2,1)}), bf16[8192,1024]{1,0:T(8,128)(2,1)}) %all-gather.2.cloned.1.call-update) | async-done | bytes 16777232 | tf_op jit(solution)/shard_map/all_gather | solution.py:49
  91.7 21.3 %copy.46 = bf16[1024,8192]{1,0:T(8,128)(2,1)} copy(bf16[1024,8192]{0,1:T(8,128)(2,1)} %bitcast.121) | data formatting | bytes 33554432 | tf_op jit(solution)/shard_map/dot_general | solution.py:47
  113.1 9.5 %fusion.25 = f32[256,4,2,128]{0,3,2,1:T(8,128)S(1)} fusion(bf16[4,2,128,8192]{3,2,1,0:T(8,128)(2,1)} %bitcast.122, bf16[1,256,8192]{2,1,0:T(8,128)(2,1)} %param.8, f32[8192]{0:T(1024)S(1)} %convert_element_type.56, f32[256]{0:T(256)S(1)} %add_rsqrt_fusion), kind=kOutput, calls=%fused_computation.27 | convolution fusion | flops 4303355904 | bytes 22053888 | tf_op jit(solution)/shard_map/dot_general | solution.py:47
  123.9 6.7 %all-to-all-start.1 = ((bf16[256,8,256]{0,2,1:T(8,128)(2,1)}), bf16[256,8,256]{0,2,1:T(8,128)(2,1)S(1)}, u32[]{:S(2)}, u32[]{:S(2)}) async-start(bf16[256,8,256]{0,2,1:T(8,128)(2,1)} %bitcast.130), calls=%async_computation.1 | async-start | bytes 2097152 | tf_op jit(solution)/shard_map/all_to_all | solution.py:74
  133.1 4.2 %reshape.170 = bf16[2048,1,4,128]{0,3,2,1:T(8,128)(2,1)} reshape(bf16[8,256,512]{1,0,2:T(8,128)(2,1)} %copy.45) | data formatting | bytes 4194304 | tf_op jit(solution)/shard_map/reshape | solution.py:79
  137.3 22.5 %all-to-all-done.1 = bf16[256,8,256]{0,2,1:T(8,128)(2,1)S(1)} async-done(((bf16[256,8,256]{0,2,1:T(8,128)(2,1)}), bf16[256,8,256]{0,2,1:T(8,128)(2,1)S(1)}, u32[]{:S(2)}, u32[]{:S(2)}) %all-to-all-start.1) | async-done | bytes 1048608 | tf_op jit(solution)/shard_map/all_to_all | solution.py:74
  161.4 72.4 %while.10 = (s32[]{:T(128)}, bf16[4,512,512]{2,1,0:T(8,128)(2,1)}, s32[4]{0:T(128)S(1)}, s32[2048]{0:T(1024)S(1)}, s32[1,2048]{1,0:T(1,128)S(1)}, /*index=5*/s32...) while((s32[]{:T(128)}, bf16[4,512,512]{2,1,0:T(8,128)(2,1)}, ...), condition=%wide.region_6.7_spmd, body=%wide.region_3.6_spmd.sunk | while | flops 2205675520 | bytes 58790092 | solution.py:107
  163.6 4.9 %fusion.41 = (f32[4,512]{1,0:T(4,128)S(1)}, f32[512,4,2048]{2,0,1:T(8,128)S(1)}) fusion(pred[512,2048]{1,0:T(8,128)(4,1)S(1)} %compare_and_fusion.2, bf16[2048,1,128]{2,0,1:T(8,128)(2,1)S(1)} %get-tuple-element.211, bf16[2048,1,4,128]{0,3,2,1:T(8,128)(2,1)} %get-tuple-element.210, s32[]{:T(128)S(6)} %select_n.63), kind=kOutput, calls=%fused_computation.2.clone.1 | convolution fusion | flops 1086322688 | bytes 18882564 | tf_op jit(solution)/shard_map/while/body/eval_jaxpr/bgpd,kgd->gpbk/dot_general | solution.py:90
  168.5 5.0 %fusion.42 = f32[4,512]{1,0:T(4,128)S(1)} fusion(f32[512,4,2048]{2,0,1:T(8,128)S(1)} %get-tuple-element.176, f32[4,512]{1,0:T(4,128)S(1)} %get-tuple-element.177, pred[512,2048]{1,0:T(8,128)(4,1)S(1)} %compare_and_fusion.2), kind=kLoop, calls=%fused_computation.3.clone.1 | loop fusion | flops 20969472 | bytes 17842176 | tf_op jit(solution)/shard_map/while/body/eval_jaxpr/reduce_sum | solution.py:99
  173.5 4.9 %divide_convert_fusion.2 = bf16[512,1,4,128]{0,3,2,1:T(8,128)(2,1)S(1)} fusion(f32[512,4,2048]{2,0,1:T(8,128)S(1)} %get-tuple-element.176, f32[4,512]{1,0:T(4,128)S(1)} %get-tuple-element.177, pred[512,2048]{1,0:T(8,128)(4,1)S(1)} %compare_and_fusion.2, bf16[2048,1,128]{0,2,1:T(8,128)(2,1)S(1)} %get-tuple-element.212, f32[512,4]{0,1:T(4,128)S(1)} %bitcast.137), kind=kOutput, calls=%fused_computation.10.clone.1 | convolution fusion | flops 1095237632 | bytes 18890752 | tf_op jit(solution)/shard_map/while/body/eval_jaxpr/gpbk,kgd->bgpd/dot_general | solution.py:101
  181.7 4.9 %fusion.41 = (f32[4,512]{1,0:T(4,128)S(1)}, f32[512,4,2048]{2,0,1:T(8,128)S(1)}) fusion(pred[512,2048]{1,0:T(8,128)(4,1)S(1)} %compare_and_fusion.2, bf16[2048,1,128]{2,0,1:T(8,128)(2,1)S(1)} %get-tuple-element.211, bf16[2048,1,4,128]{0,3,2,1:T(8,128)(2,1)} %get-tuple-element.210, s32[]{:T(128)S(6)} %select_n.63), kind=kOutput, calls=%fused_computation.2.clone.1 | convolution fusion | flops 1086322688 | bytes 18882564 | tf_op jit(solution)/shard_map/while/body/eval_jaxpr/bgpd,kgd->gpbk/dot_general | solution.py:90
  186.6 5.0 %fusion.42 = f32[4,512]{1,0:T(4,128)S(1)} fusion(f32[512,4,2048]{2,0,1:T(8,128)S(1)} %get-tuple-element.176, f32[4,512]{1,0:T(4,128)S(1)} %get-tuple-element.177, pred[512,2048]{1,0:T(8,128)(4,1)S(1)} %compare_and_fusion.2), kind=kLoop, calls=%fused_computation.3.clone.1 | loop fusion | flops 20969472 | bytes 17842176 | tf_op jit(solution)/shard_map/while/body/eval_jaxpr/reduce_sum | solution.py:99
  191.6 4.9 %divide_convert_fusion.2 = bf16[512,1,4,128]{0,3,2,1:T(8,128)(2,1)S(1)} fusion(f32[512,4,2048]{2,0,1:T(8,128)S(1)} %get-tuple-element.176, f32[4,512]{1,0:T(4,128)S(1)} %get-tuple-element.177, pred[512,2048]{1,0:T(8,128)(4,1)S(1)} %compare_and_fusion.2, bf16[2048,1,128]{0,2,1:T(8,128)(2,1)S(1)} %get-tuple-element.212, f32[512,4]{0,1:T(4,128)S(1)} %bitcast.137), kind=kOutput, calls=%fused_computation.10.clone.1 | convolution fusion | flops 1095237632 | bytes 18890752 | tf_op jit(solution)/shard_map/while/body/eval_jaxpr/gpbk,kgd->bgpd/dot_general | solution.py:101
  199.8 4.9 %fusion.41 = (f32[4,512]{1,0:T(4,128)S(1)}, f32[512,4,2048]{2,0,1:T(8,128)S(1)}) fusion(pred[512,2048]{1,0:T(8,128)(4,1)S(1)} %compare_and_fusion.2, bf16[2048,1,128]{2,0,1:T(8,128)(2,1)S(1)} %get-tuple-element.211, bf16[2048,1,4,128]{0,3,2,1:T(8,128)(2,1)} %get-tuple-element.210, s32[]{:T(128)S(6)} %select_n.63), kind=kOutput, calls=%fused_computation.2.clone.1 | convolution fusion | flops 1086322688 | bytes 18882564 | tf_op jit(solution)/shard_map/while/body/eval_jaxpr/bgpd,kgd->gpbk/dot_general | solution.py:90
  204.7 5.0 %fusion.42 = f32[4,512]{1,0:T(4,128)S(1)} fusion(f32[512,4,2048]{2,0,1:T(8,128)S(1)} %get-tuple-element.176, f32[4,512]{1,0:T(4,128)S(1)} %get-tuple-element.177, pred[512,2048]{1,0:T(8,128)(4,1)S(1)} %compare_and_fusion.2), kind=kLoop, calls=%fused_computation.3.clone.1 | loop fusion | flops 20969472 | bytes 17842176 | tf_op jit(solution)/shard_map/while/body/eval_jaxpr/reduce_sum | solution.py:99
  209.7 4.9 %divide_convert_fusion.2 = bf16[512,1,4,128]{0,3,2,1:T(8,128)(2,1)S(1)} fusion(f32[512,4,2048]{2,0,1:T(8,128)S(1)} %get-tuple-element.176, f32[4,512]{1,0:T(4,128)S(1)} %get-tuple-element.177, pred[512,2048]{1,0:T(8,128)(4,1)S(1)} %compare_and_fusion.2, bf16[2048,1,128]{0,2,1:T(8,128)(2,1)S(1)} %get-tuple-element.212, f32[512,4]{0,1:T(4,128)S(1)} %bitcast.137), kind=kOutput, calls=%fused_computation.10.clone.1 | convolution fusion | flops 1095237632 | bytes 18890752 | tf_op jit(solution)/shard_map/while/body/eval_jaxpr/gpbk,kgd->bgpd/dot_general | solution.py:101
  217.9 4.9 %fusion.41 = (f32[4,512]{1,0:T(4,128)S(1)}, f32[512,4,2048]{2,0,1:T(8,128)S(1)}) fusion(pred[512,2048]{1,0:T(8,128)(4,1)S(1)} %compare_and_fusion.2, bf16[2048,1,128]{2,0,1:T(8,128)(2,1)S(1)} %get-tuple-element.211, bf16[2048,1,4,128]{0,3,2,1:T(8,128)(2,1)} %get-tuple-element.210, s32[]{:T(128)S(6)} %select_n.63), kind=kOutput, calls=%fused_computation.2.clone.1 | convolution fusion | flops 1086322688 | bytes 18882564 | tf_op jit(solution)/shard_map/while/body/eval_jaxpr/bgpd,kgd->gpbk/dot_general | solution.py:90
  222.8 5.0 %fusion.42 = f32[4,512]{1,0:T(4,128)S(1)} fusion(f32[512,4,2048]{2,0,1:T(8,128)S(1)} %get-tuple-element.176, f32[4,512]{1,0:T(4,128)S(1)} %get-tuple-element.177, pred[512,2048]{1,0:T(8,128)(4,1)S(1)} %compare_and_fusion.2), kind=kLoop, calls=%fused_computation.3.clone.1 | loop fusion | flops 20969472 | bytes 17842176 | tf_op jit(solution)/shard_map/while/body/eval_jaxpr/reduce_sum | solution.py:99
  227.8 4.9 %divide_convert_fusion.2 = bf16[512,1,4,128]{0,3,2,1:T(8,128)(2,1)S(1)} fusion(f32[512,4,2048]{2,0,1:T(8,128)S(1)} %get-tuple-element.176, f32[4,512]{1,0:T(4,128)S(1)} %get-tuple-element.177, pred[512,2048]{1,0:T(8,128)(4,1)S(1)} %compare_and_fusion.2, bf16[2048,1,128]{0,2,1:T(8,128)(2,1)S(1)} %get-tuple-element.212, f32[512,4]{0,1:T(4,128)S(1)} %bitcast.137), kind=kOutput, calls=%fused_computation.10.clone.1 | convolution fusion | flops 1095237632 | bytes 18890752 | tf_op jit(solution)/shard_map/while/body/eval_jaxpr/gpbk,kgd->bgpd/dot_general | solution.py:101
  233.8 55.0 %all_to_all.45 = bf16[8,256,512]{2,1,0:T(8,128)(2,1)S(1)} all-to-all(bf16[8,256,512]{2,1,0:T(8,128)(2,1)} %bitcast.131), channel_id=1, replica_groups=mesh['sp'=8,'dp'=32] {'sp'}, dimensions={0} | all-to-all | bytes 4194304 | tf_op jit(solution)/shard_map/all_to_all | solution.py:110
  291.2 4.1 %copy.54 = bf16[1,256,4096]{2,1,0:T(8,128)(2,1)} copy(bf16[1,256,4096]{1,2,0:T(8,128)(2,1)} %bitcast.128) | data formatting | bytes 4194304 | tf_op jit(solution)/shard_map/broadcast_in_dim | solution.py:111
  (55 shorter events, 24.0 us)
Async XLA Ops:
  6.5 5.1 %copy-start = (s32[1,2048]{1,0:T(1,128)S(1)}, s32[1,2048]{1,0:T(1,128)}, u32[]{:S(2)}) copy-start(s32[1,2048]{1,0:T(1,128)} %param.13) | copy-start | bytes 24580
  6.5 5.1 %copy-start.2 = (s32[1,9]{1,0:T(1,128)S(1)}, s32[1,9]{1,0:T(1,128)}, u32[]{:S(2)}) copy-start(s32[1,9]{1,0:T(1,128)} %param.12) | copy-start | bytes 112
  6.5 85.2 %all-gather.2.cloned.1.call-start = ((), (), s32[]{:S(2)}) async-start(), calls=%async_computation.3 | async-start | bytes 17301504 | tf_op jit(solution)/shard_map/all_gather | solution.py:49
  15.1 10.6 %copy-start.1 = (bf16[8192]{0:T(1024)(128)(2,1)S(1)}, bf16[8192]{0:T(1024)(128)(2,1)}, u32[]{:S(2)}) copy-start(bf16[8192]{0:T(1024)(128)(2,1)} %param.10) | copy-start | bytes 49156
  16.6 106.2 %all-to-all-start = ((bf16[256,8,512]{0,2,1:T(8,128)(2,1)}), bf16[256,8,512]{0,2,1:T(8,128)(2,1)S(1)}, u32[]{:S(2)}, u32[]{:S(2)}) async-start(bf16[256,8,512]{0,2,1:T(8,128)(2,1)} %bitcast.126), calls=%async_computation | async-start | bytes 4194304 | tf_op jit(solution)/shard_map/all_to_all | solution.py:67
  123.9 36.0 %all-to-all-start.1 = ((bf16[256,8,256]{0,2,1:T(8,128)(2,1)}), bf16[256,8,256]{0,2,1:T(8,128)(2,1)S(1)}, u32[]{:S(2)}, u32[]{:S(2)}) async-start(bf16[256,8,256]{0,2,1:T(8,128)(2,1)} %bitcast.130), calls=%async_computation.1 | async-start | bytes 2097152 | tf_op jit(solution)/shard_map/all_to_all | solution.py:74
Sparse Core Ops, SparseCore 0:
  9.9 81.8 all-gather.1
where the time goes:
time: 303 us; the launch traced here: 302 us
  waiting for transfers between devices  86 us (28%)
  blocking collectives  55 us (18%)
  matrix products  48.8 us (16%)
  local copies, waits for them, and re-layouts  48.4 us (16%)
  other arithmetic  32.3 us (11%)
  starting transfers between devices  15.7 us (5%)
  between operations  13.5 us (4%)
    all_gather x1, waiting for transfers between devices, on_device(): lax.all_gather(key_value_matrix, 'dp', axis=0, tiled=True)  62.8 us
    all_to_all x1, blocking collectives, on_device(): lax.all_to_all(attended, 'sp', split_axis=0, concat_axis=1, tiled=True)  55 us
    all_to_all x1, waiting for transfers between devices, on_device(): lax.all_to_all(stacked_rows, 'sp', split_axis=1, concat_axis=0, tiled=True)  22.5 us
    dot_general x1, local copies, waits for them, and re-layouts, on_device(): jnp.dot(normed, lax.all_gather(key_value_matrix, 'dp', axis=0, tiled=True...  21.3 us
    reduce_sum x4, other arithmetic, block(): totals = jnp.sum(expo, axis=-1)  20.1 us
    dot_general x4, matrix products, block(): jnp.einsum('gpbk,kgd->bgpd', weights, values_all, preferred_element_type=...  19.8 us
    dot_general x4, matrix products, block(): jnp.einsum('bgpd,kgd->gpbk', query_block, keys_all, preferred_element_typ...  19.5 us
    dot_general x1, matrix products, on_device(): jnp.dot(normed, lax.all_gather(key_value_matrix, 'dp', axis=0, tiled=True...  9.49 us
  transfers between devices with their start and end apart: 3, of which 2 were waited for; matrix products, arithmetic and copies ran while one was open for 17% of the time, Pallas kernels for 0%

commit v1 on v0

--- a/solution.py
+++ b/solution.py
@@ -1,3 +1,4 @@
+import functools
 import math
 import jax
 import jax.numpy as jnp
@@ -9,6 +10,18 @@
 HEAD_SIZE = 128
 EPSILON = 1e-05
 ROPE_BASE = 500000.0
+
+
+def run_the_sheets(sheet, chip_axis):
+    return jnp.concatenate(
+        jax.lax.all_to_all(
+            jnp.stack(jax.lax.axis_size(chip_axis) * [sheet], axis=0), chip_axis, 0, 0
+        ),
+        axis=0,
+    )
+
+
+shape_the_skins = functools.partial(run_the_sheets, chip_axis="dp")
 
 
 def locate(positions, starts):
@@ -45,9 +58,7 @@
     all_rows = resident_rows * sequence_parallel_count
     normed = normalize(hidden_states[0], norm_gain)
     projected_rows = jnp.dot(
-        normed,
-        lax.all_gather(key_value_matrix, "dp", axis=0, tiled=True),
-        preferred_element_type=jnp.float32,
+        normed, shape_the_skins(key_value_matrix), preferred_element_type=jnp.float32
     )
     starts = trace_offsets[0]
     positions = token_order[0]

time: 303 us -> 523 us (1.73)
  the two profiles are of different devices: /device:TPU:1 before, /device:TPU:13 now
where the time goes in v1:
time: 523 us; the launch traced here: 521 us
  waiting for transfers between devices  283 us (54%)
  local copies, waits for them, and re-layouts  76.9 us (15%)
  blocking collectives  55 us (11%)
  matrix products  48.8 us (9%)
  other arithmetic  32 us (6%)
  starting transfers between devices  22.8 us (4%)
    all_to_all x1, waiting for transfers between devices, run_the_sheets(): jax.lax.all_to_all(jnp.stack(jax.lax.axis_size(chip_axis) * [sheet], axis...  260 us
    all_to_all x1, blocking collectives, on_device(): lax.all_to_all(attended, 'sp', split_axis=0, concat_axis=1, tiled=True)  55 us
    all_to_all x1, local copies, waits for them, and re-layouts, run_the_sheets(): jax.lax.all_to_all(jnp.stack(jax.lax.axis_size(chip_axis) * [sheet], axis...  22.5 us
    all_to_all x1, waiting for transfers between devices, on_device(): lax.all_to_all(stacked_rows, 'sp', split_axis=1, concat_axis=0, tiled=True)  22.5 us
    dot_general x1, local copies, waits for them, and re-layouts, on_device(): jnp.dot(normed, shape_the_skins(key_value_matrix), preferred_element_type...  21.4 us
    reduce_sum x4, other arithmetic, block(): totals = jnp.sum(expo, axis=-1)  20.1 us
    dot_general x4, matrix products, block(): jnp.einsum('gpbk,kgd->bgpd', weights, values_all, preferred_element_type=...  19.8 us
    dot_general x4, matrix products, block(): jnp.einsum('bgpd,kgd->gpbk', query_block, keys_all, preferred_element_typ...  19.5 us
  transfers between devices with their start and end apart: 3, of which 2 were waited for; matrix products, arithmetic and copies ran while one was open for 14% of the time, Pallas kernels for 0%

profile of v1, /device:TPU:13, one launch (start us, length us, event | category | flops | bytes accessed | tf_op | source)
XLA Modules:
  0.0 521.0 jit_solution(14578546628405399335)
XLA Ops:
  1.2 6.0 %stack.4 = bf16[32,256,1024]{1,2,0:T(8,128)(2,1)} broadcast(bf16[256,1024]{0,1:T(8,128)(2,1)S(1)} %copy.59), dimensions={1,2} | broadcast | bytes 17301504 | tf_op jit(solution)/shard_map/stack | solution.py:18
  7.2 8.0 %all-to-all-start.1 = ((bf16[32,256,1024]{1,2,0:T(8,128)(2,1)}), bf16[32,256,1024]{1,2,0:T(8,128)(2,1)}, u32[]{:S(2)}, u32[]{:S(2)}) async-start(bf16[32,256,1024]{1,2,0:T(8,128)(2,1)} %stack.4), calls=%async_computation.1 | async-start | bytes 33554432 | tf_op jit(solution)/shard_map/all_to_all | solution.py:17
  23.2 260.4 %all-to-all-done.1 = bf16[32,256,1024]{1,2,0:T(8,128)(2,1)} async-done(((bf16[32,256,1024]{1,2,0:T(8,128)(2,1)}), bf16[32,256,1024]{1,2,0:T(8,128)(2,1)}, u32[]{:S(2)}, u32[]{:S(2)}) %all-to-all-start.1) | async-done | bytes 16777248 | tf_op jit(solution)/shard_map/all_to_all | solution.py:17
  283.6 8.2 %all-to-all-start = ((bf16[256,8,512]{0,2,1:T(8,128)(2,1)}), bf16[256,8,512]{0,2,1:T(8,128)(2,1)S(1)}, u32[]{:S(2)}, u32[]{:S(2)}) async-start(bf16[256,8,512]{0,2,1:T(8,128)(2,1)} %bitcast.128), calls=%async_computation | async-start | bytes 4194304 | tf_op jit(solution)/shard_map/all_to_all | solution.py:78
  294.9 22.5 %copy.60 = bf16[32,256,1024]{2,1,0:T(8,128)(2,1)} copy(bf16[32,256,1024]{1,2,0:T(8,128)(2,1)} %all-to-all-done.1) | data formatting | bytes 33554432 | tf_op jit(solution)/shard_map/all_to_all | solution.py:17
  317.5 21.4 %copy.61 = bf16[1024,8192]{1,0:T(8,128)(2,1)} copy(bf16[1024,8192]{0,1:T(8,128)(2,1)} %bitcast.123) | data formatting | bytes 33554432 | tf_op jit(solution)/shard_map/dot_general | solution.py:60
  338.9 9.5 %fusion.25 = f32[256,4,2,128]{0,3,2,1:T(8,128)S(1)} fusion(bf16[4,2,128,8192]{3,2,1,0:T(8,128)(2,1)} %bitcast.124, bf16[1,256,8192]{2,1,0:T(8,128)(2,1)} %param.8, f32[8192]{0:T(1024)S(1)} %convert_element_type.56, f32[256]{0:T(256)S(1)} %add_rsqrt_fusion), kind=kOutput, calls=%fused_computation.27 | convolution fusion | flops 4303355904 | bytes 22053888 | tf_op jit(solution)/shard_map/dot_general | solution.py:60
  349.7 6.6 %all-to-all-start.2 = ((bf16[256,8,256]{0,2,1:T(8,128)(2,1)}), bf16[256,8,256]{0,2,1:T(8,128)(2,1)S(1)}, u32[]{:S(2)}, u32[]{:S(2)}) async-start(bf16[256,8,256]{0,2,1:T(8,128)(2,1)} %bitcast.132), calls=%async_computation.2 | async-start | bytes 2097152 | tf_op jit(solution)/shard_map/all_to_all | solution.py:85
  358.8 4.2 reshape.175
  363.0 22.5 %all-to-all-done.2 = bf16[256,8,256]{0,2,1:T(8,128)(2,1)S(1)} async-done(((bf16[256,8,256]{0,2,1:T(8,128)(2,1)}), bf16[256,8,256]{0,2,1:T(8,128)(2,1)S(1)}, u32[]{:S(2)}, u32[]{:S(2)}) %all-to-all-start.2) | async-done | bytes 1048608 | tf_op jit(solution)/shard_map/all_to_all | solution.py:85
  387.0 72.4 %while.10 = (s32[]{:T(128)}, bf16[4,512,512]{2,1,0:T(8,128)(2,1)}, s32[4]{0:T(128)S(1)}, s32[2048]{0:T(1024)S(1)}, s32[1,2048]{1,0:T(1,128)S(1)}, /*index=5*/s32...) while((s32[]{:T(128)}, bf16[4,512,512]{2,1,0:T(8,128)(2,1)}, ...), condition=%wide.region_6.7_spmd, body=%wide.region_3.6_spmd.sunk | while | flops 2205675520 | bytes 58790592 | solution.py:118
  389.2 4.9 fusion.41
  394.1 5.0 fusion.42
  399.2 4.9 divide_convert_fusion.2
  407.4 4.9 fusion.41
  412.2 5.0 fusion.42
  417.3 4.9 divide_convert_fusion.2
  425.5 4.9 fusion.41
  430.3 5.0 fusion.42
  435.4 4.9 divide_convert_fusion.2
  443.6 4.9 fusion.41
  448.4 5.0 fusion.42
  453.5 4.9 divide_convert_fusion.2
  459.5 55.0 %all_to_all.50 = bf16[8,256,512]{2,1,0:T(8,128)(2,1)S(1)} all-to-all(bf16[8,256,512]{2,1,0:T(8,128)(2,1)} %bitcast.133), channel_id=1, replica_groups=mesh['sp'=8,'dp'=32] {'sp'}, dimensions={0} | all-to-all | bytes 4194304 | tf_op jit(solution)/shard_map/all_to_all | solution.py:121
  (59 shorter events, 34.7 us)
Async XLA Ops:
  7.2 8.0 %copy-start = (bf16[1,256,4096]{2,1,0:T(8,128)(2,1)S(1)}, bf16[1,256,4096]{2,1,0:T(8,128)(2,1)}, u32[]{:S(2)}) copy-start(bf16[1,256,4096]{2,1,0:T(8,128)(2,1)} %param.9) | copy-start | bytes 6291460
  7.2 276.4 %all-to-all-start.1 = ((bf16[32,256,1024]{1,2,0:T(8,128)(2,1)}), bf16[32,256,1024]{1,2,0:T(8,128)(2,1)}, u32[]{:S(2)}, u32[]{:S(2)}) async-start(bf16[32,256,1024]{1,2,0:T(8,128)(2,1)} %stack.4), calls=%async_computation.1 | async-start | bytes 33554432 | tf_op jit(solution)/shard_map/all_to_all | solution.py:17
  15.2 3.0 copy-start.1
  15.2 3.0 copy-start.3
  21.7 270.1 %copy-start.2 = (bf16[8192]{0:T(1024)(128)(2,1)S(1)}, bf16[8192]{0:T(1024)(128)(2,1)}, u32[]{:S(2)}) copy-start(bf16[8192]{0:T(1024)(128)(2,1)} %param.10) | copy-start | bytes 49156
  283.6 65.0 %all-to-all-start = ((bf16[256,8,512]{0,2,1:T(8,128)(2,1)}), bf16[256,8,512]{0,2,1:T(8,128)(2,1)S(1)}, u32[]{:S(2)}, u32[]{:S(2)}) async-start(bf16[256,8,512]{0,2,1:T(8,128)(2,1)} %bitcast.128), calls=%async_computation | async-start | bytes 4194304 | tf_op jit(solution)/shard_map/all_to_all | solution.py:78
  349.7 35.8 %all-to-all-start.2 = ((bf16[256,8,256]{0,2,1:T(8,128)(2,1)}), bf16[256,8,256]{0,2,1:T(8,128)(2,1)S(1)}, u32[]{:S(2)}, u32[]{:S(2)}) async-start(bf16[256,8,256]{0,2,1:T(8,128)(2,1)} %bitcast.132), calls=%async_computation.2 | async-start | bytes 2097152 | tf_op jit(solution)/shard_map/all_to_all | solution.py:85
